TPU v7x, 512 devices: a whole 4x8x8 slice. The times are simulated.
512 devices in a mesh: comp: 2 (over x_lo), tile: 128 (over z, x_hi, y), lev: 2 (over core).
Axes of the slice: x: 4 (x_hi: 2, x_lo: 2; x = x_hi * 2 + x_lo), y: 8, z: 8, core: 2. Of those that a mesh axis runs over, the one named last changes fastest.
Arguments:
- adj_final: float32 [2, 72, 32768], P('comp', 'lev', 'tile'), may hold values from -6 to 6
- flipped_vertical_steppers: float32 [2, 72, 72], P('comp', 'lev'), as said below
- profiles: float32 [2, 6, 72], P('comp', None, 'lev'), may hold values from -0.9 to 0.9
- skin_sensitivity_pair: float32 [2, 72], P('comp', 'lev'), may hold values from -0.9 to 0.9
- match: int32 [128], replicated, may hold values from 0 to 127, each once
- remap_offs: int32 [256, 4], P('tile'), may hold values from 0 to 5
- remap_count: int32 [256], P('tile'), may hold values from 1 to 4, as said below
- conserving_transfer_factors: float32 [256, 4, 128, 128], P('tile'), may hold values from -0.25 to 0.25
Outputs:
- adj_initial: float32 [2, 72, 32768], P('comp', 'lev', 'tile')
Inputs may be any that keep to these rules, and one draw needn't show every extreme that they name: `match`: the atmosphere tiles in some order, each once. `remap_offs`: entries at or past a row block's count are to be ignored. `remap_count`: some row block uses all 4 entries. `flipped_vertical_steppers`: off-diagonal entries weigh about as much as the diagonal in each row.
All inputs are finite; a program needn't handle non-finite values.
Results may differ from a plain program's by a relative error of at most 0.00014.
Values sent between devices are 32-bit elements; how exact they have to be, the bound alone decides.
A program may use at most 64 MiB of HBM per device.

v0:
```python
import jax
import jax.numpy as jnp
from jax import lax
from jax.sharding import PartitionSpec as P

STEPS = 6
NBMAX = 4
HIGH_ACCURACY = lax.Precision.HIGHEST


def passed_along(block, axis, distance):
    devices = range(lax.axis_size(axis))
    route = [(i - distance, i) for i in devices if i - distance in devices]
    return lax.ppermute(block, axis, route)


def hit_rows(target, count):
    spots = lax.broadcasted_iota(jnp.int32, (count, target.shape[0]), 0)
    return (spots == target[None, :]).astype(jnp.float32)


def level_adder(operator):

    def add_piece(total, piece, start):
        return jnp.dot(operator, piece, precision=HIGH_ACCURACY, preferred_element_type=jnp.float32)

    return add_piece


def on_device(
    adj_final,
    flipped_vertical_steppers,
    profiles,
    skin_sensitivity_pair,
    match,
    remap_offs,
    remap_count,
    conserving_transfer_factors,
):
    tile_blocks = remap_offs.shape[0]
    block = conserving_transfer_factors.shape[2]
    grid_cells = adj_final.shape[2]
    tiles = lax.axis_size("tile")
    blocks = tiles * tile_blocks
    entries = tile_blocks * NBMAX
    own_state = adj_final[0]
    operator = flipped_vertical_steppers[0]
    flux_rows = profiles[0]
    skin_factor_vector = skin_sensitivity_pair[0]
    add_levels = level_adder(operator)
    first_block = (match[lax.axis_index("tile")] - 1) * tile_blocks
    target = jnp.mod(first_block + remap_offs, blocks).reshape(entries)
    in_use = (
        lax.broadcasted_iota(jnp.int32, (tile_blocks, NBMAX), 1) < remap_count[:, None]
    ).astype(jnp.float32)
    partial_flux = jnp.dot(flux_rows, own_state, precision=HIGH_ACCURACY)
    phi_ocn = lax.psum(partial_flux, "lev")
    phi_rows = phi_ocn.reshape(STEPS, tile_blocks, block).transpose(1, 0, 2)
    contrib = (
        jnp.einsum("reij,rsi->resj", conserving_transfer_factors, phi_rows, precision=HIGH_ACCURACY)
        * in_use[:, :, None, None]
    )
    flat = contrib.reshape(entries, STEPS * block)
    mine = lax.psum_scatter(
        jnp.dot(
            hit_rows(target, tile_blocks * lax.axis_size("tile")), flat, precision=HIGH_ACCURACY
        ),
        "tile",
        scatter_dimension=0,
        tiled=True,
    )
    flux_atm = mine.reshape(tile_blocks, STEPS, block).transpose(1, 0, 2).reshape(STEPS, grid_cells)
    flux_atm = passed_along(flux_atm, "comp", -1)
    adjoint = own_state
    surface_part = jnp.zeros((grid_cells,), jnp.float32)
    for step in reversed(range(STEPS)):
        flux_now = flux_atm[step]
        adjoint = adjoint + flux_rows[step][:, None] * flux_now[None, :]
        surface_part = surface_part + jnp.dot(skin_factor_vector, adjoint, precision=HIGH_ACCURACY)
        adjoint = add_levels(
            jnp.zeros_like(adjoint),
            lax.all_gather(adjoint, "lev", axis=0, tiled=True),
            jnp.int32(0),
        )
    marine_share = add_levels(
        jnp.zeros_like(own_state),
        lax.all_gather(own_state, "lev", axis=0, tiled=True),
        jnp.int32(0),
    )
    surface_adj = lax.psum(surface_part, "lev")
    surface_adj = passed_along(surface_adj, "comp", 1)
    piece = lax.all_gather(surface_adj.reshape(tile_blocks, block), "tile", axis=0, tiled=True)
    hits = (
        target[:, None] == lax.broadcasted_iota(jnp.int32, (entries, piece.shape[0]), 1)
    ).astype(jnp.float32)
    chosen_tile_matrices = jnp.dot(hits, piece, precision=HIGH_ACCURACY)
    chosen_tile_matrices = (
        chosen_tile_matrices.reshape(tile_blocks, NBMAX, block) * in_use[:, :, None]
    )
    marine_skin_warmth = jnp.einsum(
        "dcfv,dcv->df", conserving_transfer_factors, chosen_tile_matrices, precision=HIGH_ACCURACY
    ).reshape(grid_cells)
    marine_tile_matrix = marine_share + skin_factor_vector[:, None] * marine_skin_warmth[None, :]
    is_atmos = lax.axis_index("comp") == 0
    return jnp.where(is_atmos, adjoint, marine_tile_matrix)[None]


def solution(mesh):
    return jax.shard_map(
        on_device,
        mesh=mesh,
        in_specs=(
            P("comp", "lev", "tile"),
            P("comp", "lev", None),
            P("comp", None, "lev"),
            P("comp", "lev"),
            P(),
            P("tile", None),
            P("tile"),
            P("tile", None, None, None),
        ),
        out_specs=P("comp", "lev", "tile"),
        check_vma=False,
    )
```

profile of v0, /device:TPU:2, one launch (start us, length us, event | category | flops | bytes accessed | tf_op | source)
XLA Modules:
  0.0 1725.5 jit_solution(2810413761851644490)
XLA Ops:
  6.5 0.7 copy-done.6
  7.3 0.6 dynamic_slice.3
  8.5 0.7 copy-done.5
  9.2 0.1 eq.24
  9.3 0.6 copy-done.7
  9.9 0.9 convolution_bitcast_fusion.6
  10.8 2.5 psum.14
  13.3 0.4 convolution_multiply_fusion
  13.7 1.3 fusion.2
  15.0 1.3 dynamic-slice
  17.0 1322.4 %all-reduce.3.cloned.1.call-done = f32[256,768]{1,0:T(8,128)} async-done(((f32[256,768]{1,0:T(8,128)}), f32[256,768]{1,0:T(8,128)}) %all-reduce.3.cloned.1.call-update) | async-done | bytes 786448
  1339.4 0.7 constant_dynamic-slice_fusion
  1340.2 3.4 collective-permute-start
  1343.5 1.9 all-gather
  1345.4 0.1 fusion.10
  1345.5 1.9 all-gather.1
  1347.3 0.7 copy-done.1
  1348.1 0.2 convolution_bitcast_fusion.5
  1348.2 0.1 fusion.13
  1348.3 1.9 all-gather.2
  1350.2 0.2 convolution_bitcast_fusion.4
  1350.4 1.9 all-gather.3
  1352.3 0.2 convolution_bitcast_fusion.3
  1352.5 0.1 fusion.17
  1352.6 1.9 all-gather.4
  1354.4 0.2 convolution_bitcast_fusion.2
  1354.6 0.1 fusion.19
  1354.7 0.6 copy-done.4
  1355.3 0.2 fusion.18
  1355.5 0.2 fusion.16
  1355.7 0.2 fusion.14
  1355.9 0.2 fusion.12
  1356.1 0.1 multiply_add_fusion.5
  1356.2 1.9 all-gather.5
  1358.1 0.2 convolution_bitcast_fusion.1
  1358.3 0.2 fusion.20
  1358.5 0.1 fusion.21
  1358.6 0.1 fusion.6
  1358.8 2.5 psum.15
  1361.2 1.3 collective-permute-start.1
  1362.5 1.9 all-gather.6
  1364.4 0.2 convolution_bitcast_fusion
  1364.6 2.1 collective-permute-done.1
  1366.7 350.3 %all-gather.7 = f32[128,2,128]{2,1,0:T(2,128)S(1)} all-gather(f32[1,2,128]{2,1,0:T(2,128)S(1)} %bitcast.160), channel_id=1, replica_groups=mesh['comp'=2,'tile'=128,'lev'=2] {'tile'}, dimensions={0}, use_global_device_ids=true | all-gather | bytes 132096 | tf_op jit(solution)/shard_map/all_gather | solution.py:92
  1717.0 0.2 fusion.49
  1717.2 0.5 fusion.61
  1717.8 0.2 fusion.1
  1718.0 0.7 copy.14
  (28 shorter events, 0.4 us)
Async XLA Ops:
  6.5 6.8 copy-start
  6.5 1332.9 %all-reduce.3.cloned.1.call-start = ((), (), s32[]{:S(2)}) async-start(), calls=%async_computation | async-start | bytes 1572864
  6.5 0.7 copy-start.6
  8.5 0.7 copy-start.5
  9.2 0.7 copy-start.3
  9.2 0.7 copy-start.7
  15.0 1328.5 %copy-start.2 = (f32[1,36,256]{2,0,1:T(1,128)S(1)}, f32[1,36,256]{2,0,1:T(1,128)}, u32[]{:S(2)}) copy-start(f32[1,36,256]{2,0,1:T(1,128)} %param.8) | copy-start | bytes 110596
  1340.2 5.2 collective-permute-start
  1347.3 0.7 copy-start.1
  1354.6 0.7 copy-start.4
  1361.2 5.5 collective-permute-start.1
Sparse Core Ops, SparseCore 0:
  15.2 1324.1 all-reduce.2
where the time goes:
time: 1730 us
  waiting for transfers between devices  1320 us (76%)
  blocking collectives  368 us (21%)
    unnamed x2, waiting for transfers between devices  1320 us
    all_gather x1, blocking collectives, on_device(): lax.all_gather(surface_adj.reshape(tile_blocks, block), 'tile', axis=0, t...  350 us
  transfers between devices with their start and end apart: 3, of which 2 were waited for; matrix products, arithmetic and copies ran while one was open for 0% of the time, Pallas kernels for 0%

commit v1 on v0

--- a/solution.py
+++ b/solution.py
@@ -89,7 +89,15 @@
     )
     surface_adj = lax.psum(surface_part, "lev")
     surface_adj = passed_along(surface_adj, "comp", 1)
-    piece = lax.all_gather(surface_adj.reshape(tile_blocks, block), "tile", axis=0, tiled=True)
+    piece = jnp.concatenate(
+        lax.all_to_all(
+            jnp.stack([surface_adj.reshape(tile_blocks, block)] * lax.axis_size("tile")),
+            "tile",
+            0,
+            0,
+        ),
+        axis=0,
+    )
     hits = (
         target[:, None] == lax.broadcasted_iota(jnp.int32, (entries, piece.shape[0]), 1)
     ).astype(jnp.float32)

time: 1730 us -> 1400 us (0.81)
  the two profiles are of different devices: /device:TPU:2 before, /device:TPU:1 now
where the time goes in v1:
time: 1400 us
  waiting for transfers between devices  1260 us (90%)
  blocking collectives  98.7 us (7%)
  between operations  14.9 us (1%)
    unnamed x2, waiting for transfers between devices  1250 us
    all_gather x6, blocking collectives, on_device(): lax.all_gather(adjoint, 'lev', axis=0, tiled=True)  85.1 us
  transfers between devices with their start and end apart: 4, of which 3 were waited for; matrix products, arithmetic and copies ran while one was open for 0% of the time, Pallas kernels for 0%

profile of v1, /device:TPU:1, one launch (start us, length us, event | category | flops | bytes accessed | tf_op | source)
XLA Modules:
  0.0 1399.1 jit_solution(14343513649921902517)
XLA Ops:
  6.5 0.7 copy-done.6
  7.3 0.6 dynamic_slice.3
  8.5 0.7 copy-done.5
  9.2 0.1 eq.40
  9.3 0.6 copy-done.7
  9.9 0.9 convolution_bitcast_fusion.6
  10.8 9.0 psum.14
  19.8 0.4 convolution_multiply_fusion
  20.2 1.4 fusion.2
  21.6 1.3 dynamic-slice
  23.5 1245.0 %all-reduce.3.cloned.1.call-done = f32[256,768]{1,0:T(8,128)} async-done(((f32[256,768]{1,0:T(8,128)}), f32[256,768]{1,0:T(8,128)}) %all-reduce.3.cloned.1.call-update) | async-done | bytes 786448
  1268.6 0.7 constant_dynamic-slice_fusion
  1269.3 1.3 collective-permute-start
  1270.6 3.5 collective-permute-done
  1274.2 75.5 %all-gather.1 = f32[2,36,256]{2,1,0:T(8,128)S(1)} all-gather(f32[1,36,256]{2,1,0:T(8,128)S(1)} %fusion.10), channel_id=1, replica_groups=mesh['comp'=2,'tile'=128,'lev'=2] {'lev'}, dimensions={0}, use_global_device_ids=true | all-gather | bytes 110592 | tf_op jit(solution)/shard_map/all_gather | solution.py:82
  1349.7 0.7 copy-done.1
  1350.5 0.2 convolution_bitcast_fusion.5
  1350.7 1.9 all-gather.2
  1352.6 0.2 convolution_bitcast_fusion.4
  1352.8 0.1 fusion.15
  1352.8 1.9 all-gather.3
  1354.7 0.2 convolution_bitcast_fusion.3
  1354.9 0.1 fusion.17
  1355.0 1.9 all-gather.4
  1356.8 0.2 convolution_bitcast_fusion.2
  1357.0 0.1 fusion.19
  1357.1 0.6 copy-done.4
  1357.7 0.2 fusion.18
  1357.9 0.2 fusion.16
  1358.1 0.2 fusion.14
  1358.3 0.2 fusion.12
  1358.5 0.1 multiply_add_fusion.5
  1358.6 1.9 all-gather.5
  1360.5 0.2 convolution_bitcast_fusion.1
  1360.7 0.1 fusion.6
  1360.8 0.2 fusion.20
  1361.1 2.5 psum.15
  1363.5 1.4 collective-permute-start.1
  1364.9 2.1 all-gather
  1367.0 0.7 stack.3
  1367.7 9.6 all-to-all-start
  1377.4 2.1 all-gather.6
  1379.5 0.2 convolution_bitcast_fusion
  1379.7 10.9 all-to-all-done
  1390.7 0.2 convolution_multiply_fusion.1
  1390.9 0.5 fusion.62
  1391.4 0.2 fusion.1
  1391.6 0.7 copy.14
  (29 shorter events, 0.4 us)
Async XLA Ops:
  6.5 13.3 copy-start
  6.5 1262.0 %all-reduce.3.cloned.1.call-start = ((), (), s32[]{:S(2)}) async-start(), calls=%async_computation.1 | async-start | bytes 1572864
  6.5 0.7 copy-start.6
  8.5 0.7 copy-start.5
  9.2 0.7 copy-start.3
  9.2 0.7 copy-start.7
  21.6 1252.5 %copy-start.2 = (f32[1,36,256]{2,0,1:T(1,128)S(1)}, f32[1,36,256]{2,0,1:T(1,128)}, u32[]{:S(2)}) copy-start(f32[1,36,256]{2,0,1:T(1,128)} %param.8) | copy-start | bytes 110596
  1269.3 4.8 collective-permute-start
  1349.7 0.7 copy-start.1
  1357.0 0.7 copy-start.4
  1363.5 3.5 collective-permute-start.1
  1367.7 22.9 %all-to-all-start = ((f32[128,2,128]{2,1,0:T(2,128)}), f32[128,2,128]{2,1,0:T(2,128)S(1)}, u32[]{:S(2)}, u32[]{:S(2)}) async-start(f32[128,2,128]{2,1,0:T(2,128)} %stack.3), calls=%async_computation | async-start | bytes 262144 | tf_op jit(solution)/shard_map/all_to_all | solution.py:93
Sparse Core Ops, SparseCore 0:
  21.7 1246.8 all-reduce.2
